TPU v7x, 512 devices: a whole 4x4x16 slice. The times are simulated.
512 devices in a mesh: row: 32 (over z_lo, x, core), col: 16 (over y, z_hi).
Axes of the slice: x: 4, y: 4, z: 16 (z_hi: 4, z_lo: 4; z = z_hi * 4 + z_lo), core: 2. Of those that a mesh axis runs over, the one named last changes fastest.
Arguments:
- features: bfloat16 [65536, 512], P(('col', 'row')), may hold values from -6 to 6
- tile_values: bfloat16 [32, 16, 6, 256, 256], P('row', 'col'), may hold values from -0.109375 to 0.109375
- tile_index: int32 [32, 16, 6], P('row', 'col'), may hold values from 0 to 127, as said below
- tile_count: int32 [32, 16], P('row', 'col'), may hold values from 1 to 6, as said below
- weight: bfloat16 [512, 512], replicated, may hold values from -0.25 to 0.25
- cotangent: bfloat16 [65536, 512], P(('row', 'col')), may hold values from -6 to 6
Outputs:
- output: bfloat16 [65536, 512], P(('row', 'col'))
- weight_grad: float32 [512, 512], replicated
Inputs may be any that keep to these rules, and one draw needn't show every extreme that they name: `tile_index`: on each device the 6 slots hold different tile numbers. `tile_count`: some device has all 6 slots live.
All inputs are finite; a program needn't handle non-finite values.
Results may differ from a plain program's by a relative error of at most 0.024.
Values may be sent and summed in bfloat16 or wider, within the bound.
A program may use at most 64 MiB of HBM per device.

v0:
```python
import math

import jax
import jax.numpy as jnp
from jax import lax
from jax.sharding import PartitionSpec as P

F = 512
BLK = 256
RBG = 8
KMAX = 6


def local(features, tile_values, tile_index, tile_count, weight, cotangent):
    gathered = lax.all_gather(features, "row", axis=0, tiled=True)
    col_groups = gathered.shape[0] // BLK
    blocks = gathered.reshape(col_groups, BLK, F)
    tile_vals = tile_values[0, 0]
    tile_ids = tile_index[0, 0]
    live_count = tile_count[0, 0]
    row_slot = tile_ids // col_groups
    col_slot = tile_ids % col_groups
    is_live = jnp.arange(KMAX, dtype=jnp.int32) < live_count
    picked = blocks[col_slot]
    products = jnp.einsum("kab,kbf->kaf", tile_vals, picked, preferred_element_type=jnp.float32)
    placing = (
        (row_slot[:, None] == jnp.arange(RBG, dtype=jnp.int32)[None, :]) & is_live[:, None]
    ).astype(jnp.float32)
    partial_value = jnp.einsum("kr,kaf->raf", placing, products)
    rounded = partial_value.reshape(RBG * BLK, F).astype(jnp.bfloat16)
    summed = lax.psum_scatter(rounded, "col", scatter_dimension=0, tiled=True).astype(jnp.float32)
    aggregated = summed.astype(jnp.bfloat16)
    preact = jnp.dot(aggregated, weight, preferred_element_type=jnp.float32)
    output = jnp.where(preact > 0, preact, jnp.expm1(jnp.minimum(preact, 0.0))).astype(jnp.bfloat16)
    slope = jnp.where(preact > 0, 1.0, jnp.exp(jnp.minimum(preact, 0.0)))
    grad_pre = (cotangent.astype(jnp.float32) * slope).astype(jnp.bfloat16)
    grad_scale = 1.0 / math.sqrt(RBG * BLK * lax.axis_size("row"))
    local_grad = jnp.dot(aggregated.T, grad_pre, preferred_element_type=jnp.float32) * grad_scale
    weight_grad = lax.psum(local_grad, ("row", "col"))
    return (output, weight_grad)


def solution(mesh):
    placed = (
        P(("col", "row"), None),
        P("row", "col", None, None, None),
        P("row", "col", None),
        P("row", "col"),
        P(),
        P(("row", "col"), None),
    )
    return jax.shard_map(
        local, mesh=mesh, in_specs=placed, out_specs=(P(("row", "col"), None), P()), check_vma=False
    )
```

profile of v0, /device:TPU:1, one launch (start us, length us, event | category | flops | bytes accessed | tf_op | source)
XLA Modules:
  0.0 697.2 jit_solution(11324662987726796787)
XLA Ops:
  7.2 0.0 copy-start
  7.2 0.0 all-gather.2.cloned.1.call-start
  7.2 0.7 all-gather.2.cloned.1.call-update
  7.9 0.0 reduce-scatter.2.cloned.1.call-start
  8.6 0.7 fusion.19
  9.3 0.7 and_select_fusion.1
  10.0 74.0 %all-gather.2.cloned.1.call-done = bf16[4096,512]{1,0:T(8,128)(2,1)} async-done(((bf16[128,512]{1,0:T(8,128)(2,1)}), bf16[4096,512]{1,0:T(8,128)(2,1)}) %all-gather.2.cloned.1.call-update) | async-done | bytes 4194320 | tf_op jit(solution)/shard_map/all_gather | solution.py:15
  84.0 2.8 gather_fusion
  86.8 0.0 copy-done
  86.8 1.8 fusion.5
  88.7 3.3 copy.9
  91.9 0.7 fusion.2
  92.6 2.0 copy.8
  94.7 0.0 copy-start.1
  94.7 0.0 reduce-scatter.2.cloned.1.call-update
  94.7 0.0 all-reduce.2.cloned.1.call-start
  94.7 124.4 %reduce-scatter.2.cloned.1.call-done = bf16[128,512]{1,0:T(8,128)(2,1)} async-done(((bf16[2048,512]{1,0:T(8,128)(2,1)}), bf16[128,512]{1,0:T(8,128)(2,1)}) %reduce-scatter.2.cloned.1.call-update) | async-done | bytes 131088 | tf_op jit(solution)/shard_map/reduce_scatter | solution.py:31
  219.1 0.0 copy-done.1
  219.2 1.9 fusion.7
  221.0 0.0 copy-done.2
  221.0 2.2 convolution_multiply_fusion
  223.2 0.0 all-reduce.2.cloned.1.call-update
  223.3 465.1 %all-reduce.2.cloned.1.call-done = f32[512,512]{1,0:T(8,128)} async-done(((f32[512,512]{1,0:T(8,128)}), f32[512,512]{1,0:T(8,128)}) %all-reduce.2.cloned.1.call-update) | async-done | bytes 1048592 | tf_op jit(solution)/shard_map/psum | solution.py:39
  688.4 2.3 copy.12
  (3 shorter events, 0.0 us)
Async XLA Ops:
  7.2 79.7 %copy-start = (bf16[1,1,6,256,256]{4,3,2,1,0:T(8,128)(2,1)S(1)}, bf16[1,1,6,256,256]{4,3,2,1,0:T(8,128)(2,1)}, u32[]{:S(2)}) copy-start(bf16[1,1,6,256,256]{4,3,2,1,0:T(8,128)(2,1)} %param.7) | copy-start | bytes 2359300
  7.2 76.8 %all-gather.2.cloned.1.call-start = ((), (), s32[]{:S(2)}) async-start(), calls=%async_computation.1 | async-start | bytes 4325376 | tf_op jit(solution)/shard_map/all_gather | solution.py:15
  7.9 211.2 %reduce-scatter.2.cloned.1.call-start = ((), (), s32[]{:S(2)}) async-start(), calls=%async_computation.2 | async-start | bytes 2228224 | tf_op jit(solution)/shard_map/reduce_scatter | solution.py:31
  94.7 124.5 %copy-start.1 = (bf16[512,512]{1,0:T(8,128)(2,1)S(1)}, bf16[512,512]{1,0:T(8,128)(2,1)}, u32[]{:S(2)}) copy-start(bf16[512,512]{1,0:T(8,128)(2,1)} %param.10) | copy-start | bytes 1572868
  94.7 126.3 %copy-start.2 = (bf16[128,512]{1,0:T(8,128)(2,1)S(1)}, bf16[128,512]{1,0:T(8,128)(2,1)}, u32[]{:S(2)}) copy-start(bf16[128,512]{1,0:T(8,128)(2,1)} %param.11) | copy-start | bytes 393220
  94.7 593.7 %all-reduce.2.cloned.1.call-start = ((), (), s32[]{:S(2)}) async-start(), calls=%async_computation.3 | async-start | bytes 2097152 | tf_op jit(solution)/shard_map/psum | solution.py:39
Sparse Core Ops, SparseCore 0:
  10.2 73.7 all-gather.1
  94.8 124.2 reduce-scatter.1
  226.1 462.2 all-reduce.1
where the time goes:
time: 697 us
  waiting for transfers between devices  664 us (95%)
  between operations  14.4 us (2%)
  local copies, waits for them, and re-layouts  10.4 us (1%)
    psum x1, waiting for transfers between devices, local(): weight_grad = lax.psum(local_grad, ('row', 'col'))  465 us
    reduce_scatter x1, waiting for transfers between devices, local(): lax.psum_scatter(rounded, 'col', scatter_dimension=0, tiled=True)  124 us
    all_gather x1, waiting for transfers between devices, local(): gathered = lax.all_gather(features, 'row', axis=0, tiled=True)  74 us
  transfers between devices with their start and end apart: 3, of which 3 were waited for; matrix products, arithmetic and copies ran while one was open for 0% of the time, Pallas kernels for 0%

commit v1 on v0

v1 whole, which is shorter than its diff:
```python
import functools
import math

import jax
import jax.numpy as jnp
from jax import lax
from jax.experimental import pallas as pl
from jax.experimental.pallas import tpu as pltpu
from jax.sharding import PartitionSpec as P

F = 512
BLK = 256
RBG = 8
KMAX = 6
CBG = 16
OWN = 128
NC = 2
FC = F // NC
MESH = pl.DeviceIdType.MESH
BF16 = jnp.bfloat16
F32 = jnp.float32


def remote(src, dst, send, recv, device):
    copy = pltpu.make_async_remote_copy(
        src_ref=src, dst_ref=dst, send_sem=send, recv_sem=recv, device_id=device, device_id_type=MESH
    )
    copy.start()


def arrived(view, sem):
    pltpu.make_async_copy(view, view, sem).wait()


def kernel(
    scale,
    features, tiles, index, count, weight, cotangent,
    output, weight_grad,
    got, tile, wts, cot, sums, part, part_l, part_r, quar, quar_l, quar_r, agg,
    grad, core_out, core_in, half, xy_in, z_out, z_in, z_all, full,
    s_local, s_z, s_l, s_r, s_top, s_bot, s_sib, s_send, s_sibsend, s_y, s_q, s_gsend, s_grecv,
):
    row, col = lax.axis_index("row"), lax.axis_index("col")
    core = lax.rem(row, 2)
    block = lax.div(row, 2)
    x, z_lo = lax.rem(block, 4), lax.div(block, 4)
    y, z_hi = lax.div(col, 4), lax.rem(col, 4)
    other = 1 - core
    chip_xy = x * 4 + y
    z = z_hi * 4 + z_lo

    def at(x_=x, y_=y, z_lo_=z_lo, z_hi_=z_hi, core_=core):
        return ((z_lo_ * 4 + x_) * 2 + core_, y_ * 4 + z_hi_)

    def at_xy(i):
        return at(x_=lax.div(i, 4), y_=lax.rem(i, 4))

    def at_z(i):
        return at(z_lo_=lax.rem(i, 4), z_hi_=lax.div(i, 4))

    sibling = at(core_=other)
    x_right, x_left = at(x_=lax.rem(x + 1, 4)), at(x_=lax.rem(x + 3, 4))

    barrier = pltpu.get_barrier_semaphore()
    pl.semaphore_signal(barrier, inc=1, device_id=sibling, device_id_type=MESH)
    for d in range(1, 16):
        pl.semaphore_signal(barrier, inc=1, device_id=at_xy(lax.rem(chip_xy + d, 16)), device_id_type=MESH)
        pl.semaphore_signal(barrier, inc=1, device_id=at_z(lax.rem(z + d, 16)), device_id_type=MESH)

    own = [
        pltpu.make_async_copy(
            features.at[pl.ds(t * 64, 64), pl.ds(j * FC, FC)],
            got[j].at[block, 2 * core + t],
            s_local.at[2 * j + t],
        )
        for j in range(NC) for t in range(2)
    ]
    later = [
        pltpu.make_async_copy(tiles.at[0, 0], tile, s_local.at[2 * NC]),
        pltpu.make_async_copy(weight, wts, s_local.at[2 * NC + 1]),
        pltpu.make_async_copy(cotangent, cot, s_local.at[2 * NC + 2]),
    ]
    for copy in own + later:
        copy.start()

    slot_row = []
    slot_col = []
    live = count[0, 0]
    for k in range(KMAX):
        number = index[0, 0, k]
        slot_row.append(jnp.where(k < live, lax.div(number, CBG), RBG))
        slot_col.append(lax.rem(number, CBG))
    rank = []
    for k in range(KMAX):
        before = jnp.int32(0)
        for m in range(KMAX):
            if m != k:
                ahead = slot_row[m] <= slot_row[k] if m < k else slot_row[m] < slot_row[k]
                before = before + jnp.where(ahead, 1, 0)
        rank.append(before)
    take, take_row, take_col = [], [], []
    for s in range(KMAX):
        picked = [jnp.where(rank[k] == s, 1, 0) for k in range(KMAX)]
        take.append(sum(k * picked[k] for k in range(KMAX)))
        take_row.append(sum(slot_row[k] * picked[k] for k in range(KMAX)))
        take_col.append(sum(slot_col[k] * picked[k] for k in range(KMAX)))
    last = []
    for r in range(RBG):
        upto = sum(jnp.where(slot_row[k] <= r, 1, 0) for k in range(KMAX))
        here = sum(jnp.where(slot_row[k] == r, 1, 0) for k in range(KMAX))
        last.append(jnp.where(here > 0, upto - 1, KMAX))

    sums[KMAX] = jnp.zeros((BLK, FC), BF16)
    for copy in own:
        copy.wait()
    pl.semaphore_wait(barrier, 31)

    def shard(j, p):
        return got[j].at[p, pl.ds(2 * core, 2)]

    def give(j, p, sems, device):
        remote(shard(j, p), shard(j, p), s_send.at[j], sems, device)

    def give_half(j, p, t, sem, device):
        piece = got[j].at[p, 2 * core + t]
        remote(piece, piece, s_send.at[j], sem, device)

    def give_sibling(j, p):
        remote(shard(j, p), shard(j, p), s_sibsend.at[j], s_sib.at[j], sibling)

    def spread(j, d):
        p = lax.rem(z_lo + d, 4) * 4 + x
        give(j, p, s_l.at[j, d], x_right)
        give(j, p, s_r.at[j, d], x_left)
        give_sibling(j, p)

    def gather_start(j):
        for d in range(1, 4):
            give(j, block, s_z.at[j, 4 - d], at(z_lo_=lax.rem(z_lo + d, 4)))
        spread(j, 0)

    def gather_z(j):
        for d in range(1, 4):
            arrived(shard(j, lax.rem(z_lo + d, 4) * 4 + x), s_z.at[j, d])
            spread(j, d)

    def gather_x(j):
        for d in range(4):
            line = lax.rem(z_lo + d, 4) * 4
            p_l, p_r = line + lax.rem(x + 3, 4), line + lax.rem(x + 1, 4)
            arrived(shard(j, p_l), s_l.at[j, d])
            give_half(j, p_l, 0, s_top.at[j, d], x_right)
            give_sibling(j, p_l)
            arrived(shard(j, p_r), s_r.at[j, d])
            give_half(j, p_r, 1, s_bot.at[j, d], x_left)
            give_sibling(j, p_r)

    def gather_end(j):
        for d in range(4):
            p = lax.rem(z_lo + d, 4) * 4 + lax.rem(x + 2, 4)
            arrived(got[j].at[p, 2 * core], s_top.at[j, d])
            arrived(got[j].at[p, 2 * core + 1], s_bot.at[j, d])
            give_sibling(j, p)
        arrived(got[j].at[:, pl.ds(2 * other, 2)], s_sib.at[j])

    def multiply(j):
        for s in range(KMAX):
            features_block = got[j][take_col[s]].reshape(BLK, FC)
            product = jnp.dot(tile[take[s]], features_block, preferred_element_type=F32)
            if s:
                product = product + jnp.where(take_row[s] == take_row[s - 1], running, 0.0)
            running = product
            sums[s] = running.astype(BF16)
        for r in range(RBG):
            part[j, r] = sums[last[r]]

    def ring_start(j, buf, from_l, from_r, me, right, left, sems):
        nxt, opp, prv = lax.rem(me + 1, 4), lax.rem(me + 2, 4), lax.rem(me + 3, 4)
        remote(buf.at[j, 2 * opp], from_l.at[j, 0], sems.at[j, 0], sems.at[j, 1], right)
        remote(buf.at[j, 2 * opp + 1], from_r.at[j, 0], sems.at[j, 0], sems.at[j, 2], left)
        remote(buf.at[j, 2 * nxt + 1], from_l.at[j, 2], sems.at[j, 0], sems.at[j, 3], right)
        remote(buf.at[j, 2 * prv], from_r.at[j, 1], sems.at[j, 0], sems.at[j, 4], left)

    def ring_turn(j, buf, from_l, from_r, me, right, left, sems):
        nxt, prv = lax.rem(me + 1, 4), lax.rem(me + 3, 4)
        arrived(from_l.at[j, 0], sems.at[j, 1])
        buf[j, 2 * nxt] = (buf[j, 2 * nxt].astype(F32) + from_l[j, 0].astype(F32)).astype(BF16)
        remote(buf.at[j, 2 * nxt], from_l.at[j, 1], sems.at[j, 0], sems.at[j, 3], right)
        arrived(from_r.at[j, 0], sems.at[j, 2])
        buf[j, 2 * prv + 1] = (buf[j, 2 * prv + 1].astype(F32) + from_r[j, 0].astype(F32)).astype(BF16)
        remote(buf.at[j, 2 * prv + 1], from_r.at[j, 2], sems.at[j, 0], sems.at[j, 4], left)

    def ring_end(j, buf, from_l, from_r, me, sems):
        arrived(from_l.at[j, pl.ds(1, 2)], sems.at[j, 3])
        arrived(from_r.at[j, pl.ds(1, 2)], sems.at[j, 4])
        return [
            buf[j, 2 * me + t].astype(F32) + from_l[j, 1 + t].astype(F32) + from_r[j, 1 + t].astype(F32)
            for t in range(2)
        ]

    ring_y = (part, part_l, part_r)
    ring_q = (quar, quar_l, quar_r)
    dev_y = (y, at(y_=lax.rem(y + 1, 4)), at(y_=lax.rem(y + 3, 4)))
    dev_q = (z_hi, at(z_hi_=lax.rem(z_hi + 1, 4)), at(z_hi_=lax.rem(z_hi + 3, 4)))

    def y_start(j):
        ring_start(j, *ring_y, *dev_y, s_y)

    def y_turn(j):
        ring_turn(j, *ring_y, *dev_y, s_y)

    def y_end(j):
        for t, value in enumerate(ring_end(j, *ring_y, y, s_y)):
            quar[j, pl.ds(4 * t, 4)] = value.astype(BF16).reshape(4, 64, FC)
        ring_start(j, *ring_q, *dev_q, s_q)

    def q_turn(j):
        ring_turn(j, *ring_q, *dev_q, s_q)

    def q_end(j):
        for t, value in enumerate(ring_end(j, *ring_q, z_hi, s_q)):
            agg[pl.ds(64 * t, 64), pl.ds(j * FC, FC)] = value.astype(BF16)

    for j in range(NC):
        gather_start(j)
    later[0].wait()
    for j in range(NC):
        gather_z(j)
        if j:
            y_turn(j - 1)
        gather_x(j)
        if j:
            y_end(j - 1)
        gather_end(j)
        multiply(j)
        y_start(j)
        if j:
            q_turn(j - 1)
    y_turn(NC - 1)
    if NC > 1:
        q_end(NC - 2)
    y_end(NC - 1)
    q_turn(NC - 1)
    q_end(NC - 1)

    later[1].wait()
    later[2].wait()
    aggregated = agg[...]
    preact = jnp.dot(aggregated, wts[...], preferred_element_type=F32)
    low = jnp.minimum(preact, 0.0)
    slope = jnp.exp(low)
    near = low * (1.0 + low * (0.5 + low * (1.0 / 6 + low * (1.0 / 24))))
    output[...] = jnp.where(preact > 0, preact, jnp.where(low > -0.03125, near, slope - 1.0)).astype(BF16)
    grad_pre = (cot[...].astype(F32) * slope).astype(BF16)
    grad[...] = scale * lax.dot_general(
        aggregated, grad_pre, (((0,), (0,)), ((), ())), preferred_element_type=F32
    )

    @pl.loop(0, 16)
    def _(i):
        for g in range(4):
            core_out[i, g] = grad[pl.ds(other * 256 + i * 16, 16), pl.ds(g * 128, 128)].astype(BF16)

    remote(core_out, core_in, s_gsend.at[0], s_grecv.at[0], sibling)
    arrived(core_in, s_grecv.at[0])

    @pl.loop(0, 16)
    def _(i):
        for g in range(4):
            mine = grad[pl.ds(core * 256 + i * 16, 16), pl.ds(g * 128, 128)]
            half[i, g] = (mine + core_in[i, g].astype(F32)).astype(BF16)

    @pl.loop(1, 16)
    def _(d):
        i = lax.rem(chip_xy + d, 16)
        remote(half.at[i], xy_in.at[chip_xy], s_gsend.at[1], s_grecv.at[1], at_xy(i))

    xy_in[chip_xy] = half[chip_xy]
    arrived(xy_in.at[pl.ds(0, 15)], s_grecv.at[1])
    total = xy_in[0].astype(F32)
    for i in range(1, 16):
        total = total + xy_in[i].astype(F32)
    z_out[...] = total.astype(BF16)

    @pl.loop(1, 16)
    def _(d):
        i = lax.rem(z + d, 16)
        remote(z_out.at[lax.rem(i, 4)], z_in.at[z], s_gsend.at[2], s_grecv.at[2], at_z(i))

    z_in[z] = z_out[z_lo]
    arrived(z_in.at[pl.ds(0, 15)], s_grecv.at[2])
    total = z_in[0].astype(F32)
    for i in range(1, 16):
        total = total + z_in[i].astype(F32)
    z_all[z_lo] = total.astype(BF16)
    for d in range(1, 4):
        remote(z_all.at[z_lo], z_all.at[z_lo], s_gsend.at[3], s_grecv.at[3], at(z_lo_=lax.rem(z_lo + d, 4)))
    arrived(z_all.at[pl.ds(0, 3)], s_grecv.at[3])
    full[core, chip_xy] = z_all[...]

    @pl.loop(1, 16)
    def _(d):
        i = lax.rem(chip_xy + d, 16)
        piece = full.at[core, chip_xy]
        remote(piece, piece, s_gsend.at[4], s_grecv.at[4], at_xy(i))

    arrived(full.at[core, pl.ds(0, 15)], s_grecv.at[4])
    remote(full.at[core], full.at[core], s_gsend.at[5], s_grecv.at[5], sibling)
    arrived(full.at[other], s_grecv.at[5])
    for k in range(2):
        @pl.loop(0, 16)
        def _(i):
            for g in range(4):
                weight_grad[pl.ds(k * 256 + i * 16, 16), pl.ds(g * 128, 128)] = full[k, i, g].astype(F32)

    for j in range(NC):
        arrived(got[j].at[pl.ds(0, 15), pl.ds(0, 2)], s_send.at[j])
        arrived(got[j].at[:, pl.ds(0, 2)], s_sibsend.at[j])
        arrived(part.at[j, pl.ds(0, 6)], s_y.at[j, 0])
        arrived(quar.at[j, pl.ds(0, 6)], s_q.at[j, 0])
    arrived(core_out, s_gsend.at[0])
    arrived(half.at[pl.ds(0, 15)], s_gsend.at[1])
    arrived(z_in.at[pl.ds(0, 15)], s_gsend.at[2])
    arrived(z_all.at[pl.ds(0, 3)], s_gsend.at[3])
    arrived(full.at[0, pl.ds(0, 15)], s_gsend.at[4])
    arrived(full.at[0], s_gsend.at[5])


def solution(mesh):
    vmem, smem, hbm = pltpu.VMEM, pltpu.SMEM, pl.ANY
    dma = pltpu.SemaphoreType.DMA

    def local(*operands):
        scale = 1.0 / math.sqrt(RBG * BLK * mesh.shape["row"])
        return pl.pallas_call(
            functools.partial(kernel, scale),
            out_shape=(
                jax.ShapeDtypeStruct((OWN, F), BF16),
                jax.ShapeDtypeStruct((F, F), F32),
            ),
            in_specs=[pl.BlockSpec(memory_space=s) for s in (hbm, hbm, smem, smem, hbm, hbm)],
            out_specs=[pl.BlockSpec(memory_space=vmem)] * 2,
            scratch_shapes=[
                [vmem((CBG, 4, 64, FC), BF16)] * NC,
                vmem((KMAX, BLK, BLK), BF16),
                vmem((F, F), BF16),
                vmem((OWN, F), BF16),
                vmem((KMAX + 1, BLK, FC), BF16),
                vmem((NC, RBG, BLK, FC), BF16),
                vmem((NC, 3, BLK, FC), BF16),
                vmem((NC, 3, BLK, FC), BF16),
                vmem((NC, 8, 64, FC), BF16),
                vmem((NC, 3, 64, FC), BF16),
                vmem((NC, 3, 64, FC), BF16),
                vmem((OWN, F), BF16),
                vmem((F, F), F32),
                vmem((16, 4, 16, 128), BF16),
                vmem((16, 4, 16, 128), BF16),
                vmem((16, 4, 16, 128), BF16),
                vmem((16, 4, 16, 128), BF16),
                vmem((4, 16, 128), BF16),
                vmem((16, 16, 128), BF16),
                vmem((4, 16, 128), BF16),
                vmem((2, 16, 4, 16, 128), BF16),
                dma((2 * NC + 3,)),
                dma((NC, 4)), dma((NC, 4)), dma((NC, 4)), dma((NC, 4)), dma((NC, 4)),
                dma((NC,)), dma((NC,)), dma((NC,)),
                dma((NC, 5)), dma((NC, 5)),
                dma((6,)), dma((6,)),
            ],
            compiler_params=pltpu.CompilerParams(
                collective_id=0, has_side_effects=True, vmem_limit_bytes=48 << 20
            ),
        )(*operands)

    placed = (
        P(("col", "row"), None),
        P("row", "col", None, None, None),
        P("row", "col", None),
        P("row", "col"),
        P(),
        P(("row", "col"), None),
    )
    return jax.shard_map(
        local, mesh=mesh, in_specs=placed, out_specs=(P(("row", "col"), None), P()), check_vma=False
    )
```

time: 697 us -> 109 us (0.16)
  waiting for transfers between devices: 664 us -> 0 us
  Pallas kernels: 0 us -> 102 us
  between operations: 14.4 us -> 1.33 us
    psum x1 -> x0, waiting for transfers between devices: 465 us -> none  [local(): weight_grad = lax.psum(local_grad, ('row', 'col'))]
    reduce_scatter x1 -> x0, waiting for transfers between devices: 124 us -> none  [local(): lax.psum_scatter(rounded, 'col', scatter_dimension=0, tiled=True)]
    pallas_call x0 -> x1, Pallas kernels: none -> 102 us  [local(): pl.pallas_call(functools.partial(kernel, scale), out_shape=(jax.ShapeDtyp...]
    all_gather x1 -> x0, waiting for transfers between devices: 74 us -> none  [local(): gathered = lax.all_gather(features, 'row', axis=0, tiled=True)]
  transfers between devices with their start and end apart: 3 -> 0, of which waited for: 3 -> 0; matrix products, arithmetic and copies ran while one was open for 0% -> 0% of each run, Pallas kernels for 0% -> 0%
where the time goes in v1:
time: 109 us
  Pallas kernels  102 us (94%)
  local copies, waits for them, and re-layouts  5.61 us (5%)
  between operations  1.33 us (1%)
    pallas_call x1, Pallas kernels, local(): pl.pallas_call(functools.partial(kernel, scale), out_shape=(jax.ShapeDtyp...  102 us
    unnamed x12, local copies, waits for them, and re-layouts  5.61 us

profile of v1, /device:TPU:1, one launch (start us, length us, event | category | flops | bytes accessed | tf_op | source)
XLA Modules:
  0.0 109.0 jit_solution(4334764953057991059)
XLA Ops:
  0.6 0.0 copy-start.4
  1.3 0.0 copy-done.4
  1.3 0.0 copy-start
  1.3 1.1 %copy-done = bf16[1,1,6,256,256]{4,3,2,1,0:T(8,128)(2,1)S(1)} copy-done((bf16[1,1,6,256,256]{4,3,2,1,0:T(8,128)(2,1)S(1)}, bf16[1,1,6,256,256]{4,3,2,1,0:T(8,128)(2,1)}, u32[]{:S(2)}) %copy-start) | copy-done | bytes 786456
  2.4 0.0 copy-start.1
  2.4 1.0 copy-done.1
  3.5 0.0 copy-start.2
  3.5 0.9 copy-done.2
  4.4 0.0 copy-start.3
  4.4 0.9 copy-done.3
  5.3 102.1 %shard_map.77 = (bf16[128,512]{1,0:T(8,128)(2,1)S(1)}, f32[512,512]{1,0:T(8,128)S(1)}) custom-call(bf16[128,512]{1,0:T(8,128)(2,1)S(1)} %copy-done.2, bf16[1,1,6,256,256]{4,3,2,1,0:T(8,128)(2,1)S(1)} %copy-done, s32[1,1,6]{2,1,0:T(1,128)S(1)} %copy-done.4, s32[1,1]{1,0:T(1,128)S(6)} %copy.10.count, bf16[512,512]{1,0:T(8,128)(2,1)S(1)} %copy-done.1, ...), custom_call_target="tpu_custom_call" | custom-call | tf_op jit(solution)/shard_map/pallas_call | solution.py:335
  107.4 0.7 copy.11
  108.0 1.0 copy.12
Async XLA Ops:
  0.6 0.7 copy-start.4
  1.3 1.1 %copy-start = (bf16[1,1,6,256,256]{4,3,2,1,0:T(8,128)(2,1)S(1)}, bf16[1,1,6,256,256]{4,3,2,1,0:T(8,128)(2,1)}, u32[]{:S(2)}) copy-start(bf16[1,1,6,256,256]{4,3,2,1,0:T(8,128)(2,1)} %tiles.1) | copy-start | bytes 2359300
  2.4 1.0 copy-start.1
  3.5 0.9 copy-start.2
  4.4 0.9 copy-start.3

commit v2 on v1

v2 whole, which is shorter than its diff:
```python
import functools
import math

import jax
import jax.numpy as jnp
from jax import lax
from jax.experimental import pallas as pl
from jax.experimental.pallas import tpu as pltpu
from jax.sharding import PartitionSpec as P

F = 512
HALF = F // 2
BLK = 256
RBG = 8
KMAX = 6
CBG = 16
OWN = 128
NC = 2
FC = HALF // NC
MESH = pl.DeviceIdType.MESH
BF16 = jnp.bfloat16
F32 = jnp.float32


def remote(src, dst, send, recv, device):
    copy = pltpu.make_async_remote_copy(
        src_ref=src, dst_ref=dst, send_sem=send, recv_sem=recv, device_id=device, device_id_type=MESH
    )
    copy.start()


def arrived(view, sem):
    pltpu.make_async_copy(view, view, sem).wait()


def plan_of(index, count):
    slot_row, slot_col = [], []
    for k in range(KMAX):
        number = index[0, 0, k]
        slot_row.append(jnp.where(k < count[0, 0], lax.div(number, CBG), RBG))
        slot_col.append(lax.rem(number, CBG))
    rank = []
    for k in range(KMAX):
        before = jnp.int32(0)
        for m in range(KMAX):
            if m != k:
                ahead = slot_row[m] <= slot_row[k] if m < k else slot_row[m] < slot_row[k]
                before = before + jnp.where(ahead, 1, 0)
        rank.append(before)
    take, take_row, take_col = [], [], []
    for s in range(KMAX):
        picked = [jnp.where(rank[k] == s, 1, 0) for k in range(KMAX)]
        take.append(sum(k * picked[k] for k in range(KMAX)))
        take_row.append(sum(slot_row[k] * picked[k] for k in range(KMAX)))
        take_col.append(sum(slot_col[k] * picked[k] for k in range(KMAX)))
    goes_on = [jnp.int32(0)] + [
        jnp.where(take_row[s] == take_row[s - 1], 1, 0) for s in range(1, KMAX)
    ]
    last = []
    for r in range(RBG):
        upto = sum(jnp.where(slot_row[k] <= r, 1, 0) for k in range(KMAX))
        here = sum(jnp.where(slot_row[k] == r, 1, 0) for k in range(KMAX))
        last.append(jnp.where(here > 0, upto - 1, KMAX))
    return take + take_col + goes_on + last


def kernel(
    scale,
    features, tiles, index, count, weight, cotangent,
    output, weight_grad,
    staged, swap, got, tile, wts, cot, plan_out, plan_in, plan_s, sums, part, part_l, part_r, quar, quar_l, quar_r, res, cross,
    mine, core_out, core_in, half, xy_in, z_out, z_in, z_all, full,
    s_local, s_plan, s_swap, s_tile, s_z, s_l, s_r, s_top, s_bot, s_send, s_y, s_q, s_cross, s_gsend, s_grecv, s_far,
):
    row, col = lax.axis_index("row"), lax.axis_index("col")
    core = lax.rem(row, 2)
    block = lax.div(row, 2)
    x, z_lo = lax.rem(block, 4), lax.div(block, 4)
    y, z_hi = lax.div(col, 4), lax.rem(col, 4)
    other = 1 - core
    chip_xy = x * 4 + y
    z = z_hi * 4 + z_lo

    def at(x_=x, y_=y, z_lo_=z_lo, z_hi_=z_hi, core_=core):
        return ((z_lo_ * 4 + x_) * 2 + core_, y_ * 4 + z_hi_)

    def at_xy(i):
        return at(x_=lax.div(i, 4), y_=lax.rem(i, 4))

    def at_z(i):
        i = lax.rem(i, 16)
        return at(z_lo_=lax.rem(i, 4), z_hi_=lax.div(i, 4))

    def turn(i, d):
        return lax.rem(i + d, 4)

    sibling = at(core_=other)
    x_right, x_left = at(x_=turn(x, 1)), at(x_=turn(x, 3))
    y_right, y_left = at(y_=turn(y, 1)), at(y_=turn(y, 3))

    barrier = pltpu.get_barrier_semaphore()
    near = [sibling, x_right, x_left, y_right, y_left] + [at_z(z + 16 + d) for d in (1, -1, 2, -2, 3, -3)]
    for device in near:
        pl.semaphore_signal(barrier, inc=1, device_id=device, device_id_type=MESH)

    own = [pltpu.make_async_copy(features, staged, s_local.at[0])]
    later = [
        pltpu.make_async_copy(tiles.at[0, 0], tile[0], s_local.at[NC]),
        pltpu.make_async_copy(weight, wts, s_local.at[NC + 1]),
        pltpu.make_async_copy(cotangent, cot, s_local.at[NC + 2]),
    ]
    own[0].start()

    plan = plan_of(index, count)
    lane = lax.broadcasted_iota(jnp.int32, (8, 128), 1)
    table = jnp.zeros((8, 128), jnp.int32)
    for i, entry in enumerate(plan):
        table = jnp.where(lane == i, entry, table)
    plan_out[...] = table
    sums[KMAX] = jnp.zeros((BLK, FC), BF16)

    def columns(whose, j):
        return staged[:, pl.ds(pl.multiple_of(whose * HALF + j * FC, FC), FC)]

    own[0].wait()
    for j in range(NC):
        swap[j] = columns(other, j)
        got[j][block, core] = columns(core, j)
    pl.semaphore_wait(barrier, 11)
    pl.semaphore_signal(s_far.at[0], inc=1, device_id=at_z(z + 13), device_id_type=MESH)
    pl.semaphore_signal(s_far.at[1], inc=1, device_id=at_z(z + 3), device_id_type=MESH)

    for j in range(NC):
        remote(swap.at[j], got[j].at[block, core], s_plan.at[2 + j], s_swap.at[j], sibling)
    remote(plan_out, plan_in, s_plan.at[0], s_plan.at[1], sibling)

    def give(j, p, sem, device):
        remote(got[j].at[p], got[j].at[p], s_send.at[j], sem, device)

    def give_half(j, p, t, sem, device):
        remote(got[j].at[p, t], got[j].at[p, t], s_send.at[j], sem, device)

    def spread(j, d):
        p = turn(z_lo, d) * 4 + x
        give(j, p, s_l.at[j, d], x_right)
        give(j, p, s_r.at[j, d], x_left)

    def gather_start(j):
        arrived(got[j].at[block, other], s_swap.at[j])
        for d in (1, 3, 2):
            give(j, block, s_z.at[j, 4 - d], at(z_lo_=turn(z_lo, d)))
        spread(j, 0)

    def gather_z(j):
        for d in range(1, 4):
            arrived(got[j].at[turn(z_lo, d) * 4 + x], s_z.at[j, d])
            spread(j, d)

    def gather_x(j, part=range(4)):
        for d in part:
            line = turn(z_lo, d) * 4
            p_l, p_r = line + turn(x, 3), line + turn(x, 1)
            arrived(got[j].at[p_l], s_l.at[j, d])
            give_half(j, p_l, 0, s_top.at[j, d], x_right)
            arrived(got[j].at[p_r], s_r.at[j, d])
            give_half(j, p_r, 1, s_bot.at[j, d], x_left)

    def gather_end(j):
        for d in range(4):
            p = turn(z_lo, d) * 4 + turn(x, 2)
            arrived(got[j].at[p, 0], s_top.at[j, d])
            arrived(got[j].at[p, 1], s_bot.at[j, d])

    def multiply(u):
        j = u // 2
        entry = (lambda i: plan_s[0, i]) if u % 2 else (lambda i: plan[i])
        for s in range(KMAX):
            features_block = got[j][entry(KMAX + s)].reshape(BLK, FC)
            product = jnp.dot(tile[u % 2][entry(s)], features_block, preferred_element_type=F32)
            if s:
                product = product + jnp.where(entry(2 * KMAX + s) == 1, running, 0.0)
            running = product
            sums[s] = running.astype(BF16)
        for r in range(RBG):
            part[u, r] = sums[entry(3 * KMAX + r)]

    def ring_start(j, buf, from_l, from_r, me, right, left, sems):
        nxt, opp, prv = turn(me, 1), turn(me, 2), turn(me, 3)
        remote(buf.at[j, 2 * opp], from_l.at[j, 0], sems.at[j, 0], sems.at[j, 1], right)
        remote(buf.at[j, 2 * opp + 1], from_r.at[j, 0], sems.at[j, 0], sems.at[j, 2], left)
        remote(buf.at[j, 2 * nxt + 1], from_l.at[j, 2], sems.at[j, 0], sems.at[j, 3], right)
        remote(buf.at[j, 2 * prv], from_r.at[j, 1], sems.at[j, 0], sems.at[j, 4], left)

    def ring_turn(j, buf, from_l, from_r, me, right, left, sems):
        nxt, prv = turn(me, 1), turn(me, 3)
        arrived(from_l.at[j, 0], sems.at[j, 1])
        buf[j, 2 * nxt] = (buf[j, 2 * nxt].astype(F32) + from_l[j, 0].astype(F32)).astype(BF16)
        remote(buf.at[j, 2 * nxt], from_l.at[j, 1], sems.at[j, 0], sems.at[j, 3], right)
        arrived(from_r.at[j, 0], sems.at[j, 2])
        buf[j, 2 * prv + 1] = (buf[j, 2 * prv + 1].astype(F32) + from_r[j, 0].astype(F32)).astype(BF16)
        remote(buf.at[j, 2 * prv + 1], from_r.at[j, 2], sems.at[j, 0], sems.at[j, 4], left)

    def ring_end(j, buf, from_l, from_r, me, sems):
        arrived(from_l.at[j, pl.ds(1, 2)], sems.at[j, 3])
        arrived(from_r.at[j, pl.ds(1, 2)], sems.at[j, 4])
        return [
            (buf[j, 2 * me + t].astype(F32) + from_l[j, 1 + t].astype(F32) + from_r[j, 1 + t].astype(F32)).astype(BF16)
            for t in range(2)
        ]

    ring_y = (part, part_l, part_r)
    ring_q = (quar, quar_l, quar_r)
    dev_y = (y, y_right, y_left)
    dev_q = (z_hi, at(z_hi_=turn(z_hi, 1)), at(z_hi_=turn(z_hi, 3)))

    def y_start(j):
        ring_start(j, *ring_y, *dev_y, s_y)

    def y_turn(j):
        ring_turn(j, *ring_y, *dev_y, s_y)

    def y_end(j):
        for t, value in enumerate(ring_end(j, *ring_y, y, s_y)):
            for q in range(4):
                quar[j, 4 * t + q] = value[q * 64:(q + 1) * 64]
        ring_start(j, *ring_q, *dev_q, s_q)

    def q_turn(j):
        ring_turn(j, *ring_q, *dev_q, s_q)

    def q_end(u):
        for t, value in enumerate(ring_end(u, *ring_q, z_hi, s_q)):
            res[u, pl.ds(64 * t, 64)] = value
        if u % 2:
            remote(res.at[u], cross.at[u // 2], s_cross.at[u // 2, 0], s_cross.at[u // 2, 1], sibling)

    gather_start(0)
    for copy in later:
        copy.start()
    later[0].wait()
    remote(tile[0], tile[1], s_tile.at[0], s_tile.at[1], sibling)
    arrived(plan_in, s_plan.at[1])
    to_scalars = pltpu.make_async_copy(plan_in, plan_s, s_local.at[NC + 3])
    to_scalars.start()
    gather_z(0)
    gather_start(1)
    gather_x(0)
    gather_z(1)
    gather_end(0)
    multiply(0)
    y_start(0)
    to_scalars.wait()
    arrived(tile[1], s_tile.at[1])
    multiply(1)
    y_start(1)
    gather_x(1, (0, 1))
    y_turn(0)
    gather_x(1, (2, 3))
    y_turn(1)
    pl.semaphore_wait(s_far.at[0], 1)
    pl.semaphore_wait(s_far.at[1], 1)
    y_end(0)
    gather_end(1)
    multiply(3)
    y_start(3)
    y_end(1)
    multiply(2)
    y_start(2)
    q_turn(0)
    y_turn(3)
    q_turn(1)
    q_end(0)
    y_turn(2)
    y_end(3)
    q_end(1)
    y_end(2)
    q_turn(3)
    q_turn(2)
    q_end(3)
    q_end(2)

    later[1].wait()
    later[2].wait()

    def rows_of(whose, j):
        return pl.ds(pl.multiple_of(whose * HALF + j * FC, FC), FC)

    kept = [res[2 * j] for j in range(NC)]
    preact = sum(jnp.dot(kept[j], wts[rows_of(core, j)], preferred_element_type=F32) for j in range(NC))
    for j in range(NC):
        arrived(cross.at[j], s_cross.at[j, 1])
    swapped = [cross[j] for j in range(NC)]
    preact = preact + sum(
        jnp.dot(swapped[j], wts[rows_of(other, j)], preferred_element_type=F32) for j in range(NC)
    )
    low = jnp.minimum(preact, 0.0)
    slope = jnp.exp(low)
    near = low * (1.0 + low * (0.5 + low * (1.0 / 6 + low * (1.0 / 24))))
    output[...] = jnp.where(preact > 0, preact, jnp.where(low > -0.03125, near, slope - 1.0)).astype(BF16)
    grad_pre = (cot[...].astype(F32) * slope).astype(BF16)

    def term(aggregated):
        return scale * lax.dot_general(
            aggregated, grad_pre, (((0,), (0,)), ((), ())), preferred_element_type=F32
        )

    span = FC // 16
    for j in range(NC):
        value = term(swapped[j]).astype(BF16)
        for g in range(4):
            core_out[pl.ds(j * span, span), g] = value[:, g * 128:(g + 1) * 128].reshape(span, 16, 128)
    remote(core_out, core_in, s_gsend.at[0], s_grecv.at[0], sibling)
    for j in range(NC):
        value = term(kept[j])
        for g in range(4):
            mine[pl.ds(j * span, span), g] = value[:, g * 128:(g + 1) * 128].reshape(span, 16, 128)
    arrived(core_in, s_grecv.at[0])
    half[...] = (mine[...] + core_in[...].astype(F32)).astype(BF16)

    for d in range(1, 16):
        i = lax.rem(chip_xy + d, 16)
        remote(half.at[i], xy_in.at[chip_xy], s_gsend.at[1], s_grecv.at[1], at_xy(i))
    xy_in[chip_xy] = half[chip_xy]
    arrived(xy_in.at[pl.ds(0, 15)], s_grecv.at[1])
    total = xy_in[0].astype(F32)
    for i in range(1, 16):
        total = total + xy_in[i].astype(F32)
    z_out[...] = total.astype(BF16)

    for d in range(1, 16):
        i = lax.rem(z + d, 16)
        remote(z_out.at[lax.rem(i, 4)], z_in.at[z], s_gsend.at[2], s_grecv.at[2], at_z(i))
    z_in[z] = z_out[z_lo]
    arrived(z_in.at[pl.ds(0, 15)], s_grecv.at[2])
    total = z_in[0].astype(F32)
    for i in range(1, 16):
        total = total + z_in[i].astype(F32)
    z_all[z_lo] = total.astype(BF16)
    for d in range(1, 4):
        remote(z_all.at[z_lo], z_all.at[z_lo], s_gsend.at[4], s_grecv.at[4], at(z_lo_=turn(z_lo, d)))
    arrived(z_all.at[pl.ds(0, 3)], s_grecv.at[4])
    full[core, chip_xy] = z_all[...]
    for d in range(1, 16):
        piece = full.at[core, chip_xy]
        remote(piece, piece, s_gsend.at[5], s_grecv.at[5], at_xy(lax.rem(chip_xy + d, 16)))
    arrived(full.at[core, pl.ds(0, 15)], s_grecv.at[5])
    remote(full.at[core], full.at[core], s_gsend.at[6], s_grecv.at[6], sibling)

    def finish(whose):
        for g in range(4):
            weight_grad[pl.ds(pl.multiple_of(whose * 256, 256), 256), pl.ds(g * 128, 128)] = (
                full[whose, :, g].reshape(256, 128).astype(F32)
            )

    finish(core)
    arrived(full.at[other], s_grecv.at[6])
    finish(other)

    arrived(plan_out, s_plan.at[0])
    arrived(tile[0], s_tile.at[0])
    for j in range(NC):
        arrived(got[j].at[block, core], s_plan.at[2 + j])
        arrived(got[j].at[pl.ds(0, 15)], s_send.at[j])
        for u in (2 * j, 2 * j + 1):
            arrived(part.at[u, pl.ds(0, 6)], s_y.at[u, 0])
            arrived(quar.at[u, pl.ds(0, 6)], s_q.at[u, 0])
        arrived(cross.at[j], s_cross.at[j, 0])
    arrived(core_out, s_gsend.at[0])
    arrived(half.at[pl.ds(0, 15)], s_gsend.at[1])
    arrived(z_in.at[pl.ds(0, 15)], s_gsend.at[2])
    arrived(z_all.at[pl.ds(0, 3)], s_gsend.at[4])
    arrived(full.at[core, pl.ds(0, 15)], s_gsend.at[5])
    arrived(full.at[core], s_gsend.at[6])


def solution(mesh):
    vmem, smem, hbm = pltpu.VMEM, pltpu.SMEM, pltpu.HBM
    dma = pltpu.SemaphoreType.DMA

    def local(*operands):
        scale = 1.0 / math.sqrt(RBG * BLK * mesh.shape["row"])
        return pl.pallas_call(
            functools.partial(kernel, scale),
            out_shape=(
                jax.ShapeDtypeStruct((OWN, F), BF16),
                jax.ShapeDtypeStruct((F, F), F32),
            ),
            in_specs=[pl.BlockSpec(memory_space=s) for s in (hbm, hbm, smem, smem, hbm, hbm)],
            out_specs=[pl.BlockSpec(memory_space=vmem)] * 2,
            scratch_shapes=[
                vmem((OWN, F), BF16),
                vmem((NC, OWN, FC), BF16),
                [vmem((CBG, 2, OWN, FC), BF16)] * NC,
                [vmem((KMAX, BLK, BLK), BF16)] * 2,
                vmem((F, F), BF16),
                vmem((OWN, F), BF16),
                vmem((8, 128), jnp.int32),
                vmem((8, 128), jnp.int32),
                smem((8, 128), jnp.int32),
                vmem((KMAX + 1, BLK, FC), BF16),
                vmem((2 * NC, RBG, BLK, FC), BF16),
                vmem((2 * NC, 3, BLK, FC), BF16),
                vmem((2 * NC, 3, BLK, FC), BF16),
                vmem((2 * NC, 8, 64, FC), BF16),
                vmem((2 * NC, 3, 64, FC), BF16),
                vmem((2 * NC, 3, 64, FC), BF16),
                vmem((2 * NC, OWN, FC), BF16),
                vmem((NC, OWN, FC), BF16),
                vmem((16, 4, 16, 128), F32),
                vmem((16, 4, 16, 128), BF16),
                vmem((16, 4, 16, 128), BF16),
                vmem((16, 4, 16, 128), BF16),
                vmem((16, 4, 16, 128), BF16),
                vmem((4, 16, 128), BF16),
                vmem((16, 16, 128), BF16),
                vmem((4, 16, 128), BF16),
                vmem((2, 16, 4, 16, 128), BF16),
                dma((NC + 4,)), dma((2 + NC,)), dma((NC,)), dma((2,)),
                dma((NC, 4)), dma((NC, 4)), dma((NC, 4)), dma((NC, 4)), dma((NC, 4)),
                dma((NC,)),
                dma((2 * NC, 5)), dma((2 * NC, 5)), dma((NC, 2)),
                dma((7,)), dma((7,)),
                pltpu.SemaphoreType.REGULAR((2,)),
            ],
            compiler_params=pltpu.CompilerParams(
                collective_id=0, has_side_effects=True, vmem_limit_bytes=48 << 20
            ),
        )(*[
            a if i in (2, 3) else pltpu.with_memory_space_constraint(a, pltpu.HBM)
            for i, a in enumerate(operands)
        ])

    placed = (
        P(("col", "row"), None),
        P("row", "col", None, None, None),
        P("row", "col", None),
        P("row", "col"),
        P(),
        P(("row", "col"), None),
    )
    return jax.shard_map(
        local, mesh=mesh, in_specs=placed, out_specs=(P(("row", "col"), None), P()), check_vma=False
    )
```

time: 109 us -> 100 us (0.917)
  Pallas kernels: 102 us -> 97.2 us
  local copies, waits for them, and re-layouts: 5.61 us -> 1.63 us
    pallas_call x1, Pallas kernels: 102 us -> 97.2 us  [local(): pl.pallas_call(functools.partial(kernel, scale), out_shape=(jax.ShapeDtyp...]
    unnamed x12 -> x4, local copies, waits for them, and re-layouts: 5.61 us -> 1.63 us
where the time goes in v2:
time: 100 us
  Pallas kernels  97.2 us (97%)
  local copies, waits for them, and re-layouts  1.63 us (2%)
  between operations  1.31 us (1%)
    pallas_call x1, Pallas kernels, local(): pl.pallas_call(functools.partial(kernel, scale), out_shape=(jax.ShapeDtyp...  97.2 us

profile of v2, /device:TPU:1, one launch (start us, length us, event | category | flops | bytes accessed | tf_op | source)
XLA Modules:
  0.0 100.2 jit_solution(13728221967317687177)
XLA Ops:
  0.6 0.0 copy-start
  1.3 0.0 copy-done
  1.3 97.2 %shard_map.77 = (bf16[128,512]{1,0:T(8,128)(2,1)S(1)}, f32[512,512]{1,0:T(8,128)S(1)}) custom-call(bf16[128,512]{1,0:T(8,128)(2,1)} %features.1, bf16[1,1,6,256,256]{4,3,2,1,0:T(8,128)(2,1)} %tiles.1, s32[1,1,6]{2,1,0:T(1,128)S(1)} %copy-done, s32[1,1]{1,0:T(1,128)S(6)} %copy.10.count, bf16[512,512]{1,0:T(8,128)(2,1)} %weight.1, bf16[128,512]{1,0:T(8,128)(2,1)} %cotangent.1), custom_call_target="tpu_custom_call" | custom-call | tf_op jit(solution)/shard_map/pallas_call | solution.py:382
  98.6 0.7 copy.11
  99.2 1.0 copy.12
Async XLA Ops:
  0.6 0.7 copy-start

commit v3 on v2

--- a/solution.py
+++ b/solution.py
@@ -66,11 +66,11 @@
 
 def kernel(
     scale,
-    features, tiles, index, count, weight, cotangent,
+    features, tiles, index_in, count, weight, cotangent,
     output, weight_grad,
     staged, swap, got, tile, wts, cot, plan_out, plan_in, plan_s, sums, part, part_l, part_r, quar, quar_l, quar_r, res, cross,
     mine, core_out, core_in, half, xy_in, z_out, z_in, z_all, full,
-    s_local, s_plan, s_swap, s_tile, s_z, s_l, s_r, s_top, s_bot, s_send, s_y, s_q, s_cross, s_gsend, s_grecv, s_far,
+    s_local, s_plan, s_swap, s_tile, s_z, s_l, s_r, s_top, s_bot, s_send, s_y, s_q, s_cross, s_gsend, s_grecv, s_far, index,
 ):
     row, col = lax.axis_index("row"), lax.axis_index("col")
     core = lax.rem(row, 2)
@@ -100,6 +100,7 @@
 
     barrier = pltpu.get_barrier_semaphore()
     near = [sibling, x_right, x_left, y_right, y_left] + [at_z(z + 16 + d) for d in (1, -1, 2, -2, 3, -3)]
+    near += [at(x_=turn(x, d), core_=other) for d in (1, 3)] + [at(z_lo_=turn(z_lo, d), core_=other) for d in (1, 2, 3)]
     for device in near:
         pl.semaphore_signal(barrier, inc=1, device_id=device, device_id_type=MESH)
 
@@ -109,14 +110,13 @@
         pltpu.make_async_copy(weight, wts, s_local.at[NC + 1]),
         pltpu.make_async_copy(cotangent, cot, s_local.at[NC + 2]),
     ]
+    scalars = [
+        pltpu.make_async_copy(index_in, index, s_local.at[NC + 4]),
+    ]
     own[0].start()
-
-    plan = plan_of(index, count)
-    lane = lax.broadcasted_iota(jnp.int32, (8, 128), 1)
-    table = jnp.zeros((8, 128), jnp.int32)
-    for i, entry in enumerate(plan):
-        table = jnp.where(lane == i, entry, table)
-    plan_out[...] = table
+    for copy in scalars:
+        copy.start()
+
     sums[KMAX] = jnp.zeros((BLK, FC), BF16)
 
     def columns(whose, j):
@@ -126,19 +126,23 @@
     for j in range(NC):
         swap[j] = columns(other, j)
         got[j][block, core] = columns(core, j)
-    pl.semaphore_wait(barrier, 11)
+    pl.semaphore_wait(barrier, 16)
     pl.semaphore_signal(s_far.at[0], inc=1, device_id=at_z(z + 13), device_id_type=MESH)
     pl.semaphore_signal(s_far.at[1], inc=1, device_id=at_z(z + 3), device_id_type=MESH)
 
-    for j in range(NC):
-        remote(swap.at[j], got[j].at[block, core], s_plan.at[2 + j], s_swap.at[j], sibling)
-    remote(plan_out, plan_in, s_plan.at[0], s_plan.at[1], sibling)
-
     def give(j, p, sem, device):
         remote(got[j].at[p], got[j].at[p], s_send.at[j], sem, device)
 
     def give_half(j, p, t, sem, device):
         remote(got[j].at[p, t], got[j].at[p, t], s_send.at[j], sem, device)
+
+    def give_own(j, sem, same, crossed):
+        remote(got[j].at[block, core], got[j].at[block, core], s_send.at[j], sem, same)
+        remote(swap.at[j], got[j].at[block, core], s_send.at[j], sem, crossed)
+
+    def spread_own(j):
+        give_own(j, s_l.at[j, 0], x_right, at(x_=turn(x, 1), core_=other))
+        give_own(j, s_r.at[j, 0], x_left, at(x_=turn(x, 3), core_=other))
 
     def spread(j, d):
         p = turn(z_lo, d) * 4 + x
@@ -146,10 +150,8 @@
         give(j, p, s_r.at[j, d], x_left)
 
     def gather_start(j):
-        arrived(got[j].at[block, other], s_swap.at[j])
         for d in (1, 3, 2):
-            give(j, block, s_z.at[j, 4 - d], at(z_lo_=turn(z_lo, d)))
-        spread(j, 0)
+            give_own(j, s_z.at[j, 4 - d], at(z_lo_=turn(z_lo, d)), at(z_lo_=turn(z_lo, d), core_=other))
 
     def gather_z(j):
         for d in range(1, 4):
@@ -166,10 +168,27 @@
             give_half(j, p_r, 1, s_bot.at[j, d], x_left)
 
     def gather_end(j):
+        arrived(got[j].at[block, other], s_swap.at[j])
         for d in range(4):
             p = turn(z_lo, d) * 4 + turn(x, 2)
             arrived(got[j].at[p, 0], s_top.at[j, d])
             arrived(got[j].at[p, 1], s_bot.at[j, d])
+
+    gather_start(0)
+    spread_own(0)
+    for j in range(NC):
+        remote(swap.at[j], got[j].at[block, core], s_plan.at[2 + j], s_swap.at[j], sibling)
+    for copy in later:
+        copy.start()
+    for copy in scalars:
+        copy.wait()
+    plan = plan_of(index, count)
+    lane = lax.broadcasted_iota(jnp.int32, (8, 128), 1)
+    table = jnp.zeros((8, 128), jnp.int32)
+    for i, entry in enumerate(plan):
+        table = jnp.where(lane == i, entry, table)
+    plan_out[...] = table
+    remote(plan_out, plan_in, s_plan.at[0], s_plan.at[1], sibling)
 
     def multiply(u):
         j = u // 2
@@ -185,20 +204,18 @@
             part[u, r] = sums[entry(3 * KMAX + r)]
 
     def ring_start(j, buf, from_l, from_r, me, right, left, sems):
-        nxt, opp, prv = turn(me, 1), turn(me, 2), turn(me, 3)
+        opp = turn(me, 2)
         remote(buf.at[j, 2 * opp], from_l.at[j, 0], sems.at[j, 0], sems.at[j, 1], right)
         remote(buf.at[j, 2 * opp + 1], from_r.at[j, 0], sems.at[j, 0], sems.at[j, 2], left)
-        remote(buf.at[j, 2 * nxt + 1], from_l.at[j, 2], sems.at[j, 0], sems.at[j, 3], right)
-        remote(buf.at[j, 2 * prv], from_r.at[j, 1], sems.at[j, 0], sems.at[j, 4], left)
 
     def ring_turn(j, buf, from_l, from_r, me, right, left, sems):
         nxt, prv = turn(me, 1), turn(me, 3)
         arrived(from_l.at[j, 0], sems.at[j, 1])
         buf[j, 2 * nxt] = (buf[j, 2 * nxt].astype(F32) + from_l[j, 0].astype(F32)).astype(BF16)
-        remote(buf.at[j, 2 * nxt], from_l.at[j, 1], sems.at[j, 0], sems.at[j, 3], right)
+        remote(buf.at[j, pl.ds(2 * nxt, 2)], from_l.at[j, pl.ds(1, 2)], sems.at[j, 0], sems.at[j, 3], right)
         arrived(from_r.at[j, 0], sems.at[j, 2])
         buf[j, 2 * prv + 1] = (buf[j, 2 * prv + 1].astype(F32) + from_r[j, 0].astype(F32)).astype(BF16)
-        remote(buf.at[j, 2 * prv + 1], from_r.at[j, 2], sems.at[j, 0], sems.at[j, 4], left)
+        remote(buf.at[j, pl.ds(2 * prv, 2)], from_r.at[j, pl.ds(1, 2)], sems.at[j, 0], sems.at[j, 4], left)
 
     def ring_end(j, buf, from_l, from_r, me, sems):
         arrived(from_l.at[j, pl.ds(1, 2)], sems.at[j, 3])
@@ -234,9 +251,6 @@
         if u % 2:
             remote(res.at[u], cross.at[u // 2], s_cross.at[u // 2, 0], s_cross.at[u // 2, 1], sibling)
 
-    gather_start(0)
-    for copy in later:
-        copy.start()
     later[0].wait()
     remote(tile[0], tile[1], s_tile.at[0], s_tile.at[1], sibling)
     arrived(plan_in, s_plan.at[1])
@@ -245,8 +259,9 @@
     gather_z(0)
     gather_start(1)
     gather_x(0)
+    spread_own(1)
+    gather_end(0)
     gather_z(1)
-    gather_end(0)
     multiply(0)
     y_start(0)
     to_scalars.wait()
@@ -255,23 +270,23 @@
     y_start(1)
     gather_x(1, (0, 1))
     y_turn(0)
-    gather_x(1, (2, 3))
     y_turn(1)
     pl.semaphore_wait(s_far.at[0], 1)
     pl.semaphore_wait(s_far.at[1], 1)
     y_end(0)
+    gather_x(1, (2, 3))
+    y_end(1)
     gather_end(1)
     multiply(3)
     y_start(3)
-    y_end(1)
     multiply(2)
     y_start(2)
     q_turn(0)
     y_turn(3)
     q_turn(1)
-    q_end(0)
     y_turn(2)
     y_end(3)
+    q_end(0)
     q_end(1)
     y_end(2)
     q_turn(3)
@@ -317,8 +332,10 @@
     arrived(core_in, s_grecv.at[0])
     half[...] = (mine[...] + core_in[...].astype(F32)).astype(BF16)
 
-    for d in range(1, 16):
-        i = lax.rem(chip_xy + d, 16)
+    hops = (0, 1, 2, 1)
+    far_first = sorted(((dx, dy) for dx in range(4) for dy in range(4)), key=lambda d: -hops[d[0]] - hops[d[1]])[:15]
+    for dx, dy in far_first:
+        i = turn(x, dx) * 4 + turn(y, dy)
         remote(half.at[i], xy_in.at[chip_xy], s_gsend.at[1], s_grecv.at[1], at_xy(i))
     xy_in[chip_xy] = half[chip_xy]
     arrived(xy_in.at[pl.ds(0, 15)], s_grecv.at[1])
@@ -327,7 +344,7 @@
         total = total + xy_in[i].astype(F32)
     z_out[...] = total.astype(BF16)
 
-    for d in range(1, 16):
+    for d in (8, 7, 9, 6, 10, 5, 11, 4, 12, 3, 13, 2, 14, 1, 15):
         i = lax.rem(z + d, 16)
         remote(z_out.at[lax.rem(i, 4)], z_in.at[z], s_gsend.at[2], s_grecv.at[2], at_z(i))
     z_in[z] = z_out[z_lo]
@@ -340,9 +357,9 @@
         remote(z_all.at[z_lo], z_all.at[z_lo], s_gsend.at[4], s_grecv.at[4], at(z_lo_=turn(z_lo, d)))
     arrived(z_all.at[pl.ds(0, 3)], s_grecv.at[4])
     full[core, chip_xy] = z_all[...]
-    for d in range(1, 16):
-        piece = full.at[core, chip_xy]
-        remote(piece, piece, s_gsend.at[5], s_grecv.at[5], at_xy(lax.rem(chip_xy + d, 16)))
+    piece = full.at[core, chip_xy]
+    for dx, dy in far_first:
+        remote(piece, piece, s_gsend.at[5], s_grecv.at[5], at(x_=turn(x, dx), y_=turn(y, dy)))
     arrived(full.at[core, pl.ds(0, 15)], s_grecv.at[5])
     remote(full.at[core], full.at[core], s_gsend.at[6], s_grecv.at[6], sibling)
 
@@ -385,7 +402,7 @@
                 jax.ShapeDtypeStruct((OWN, F), BF16),
                 jax.ShapeDtypeStruct((F, F), F32),
             ),
-            in_specs=[pl.BlockSpec(memory_space=s) for s in (hbm, hbm, smem, smem, hbm, hbm)],
+            in_specs=[pl.BlockSpec(memory_space=s) for s in (hbm, hbm, hbm, smem, hbm, hbm)],
             out_specs=[pl.BlockSpec(memory_space=vmem)] * 2,
             scratch_shapes=[
                 vmem((OWN, F), BF16),
@@ -415,18 +432,19 @@
                 vmem((16, 16, 128), BF16),
                 vmem((4, 16, 128), BF16),
                 vmem((2, 16, 4, 16, 128), BF16),
-                dma((NC + 4,)), dma((2 + NC,)), dma((NC,)), dma((2,)),
+                dma((NC + 5,)), dma((2 + NC,)), dma((NC,)), dma((2,)),
                 dma((NC, 4)), dma((NC, 4)), dma((NC, 4)), dma((NC, 4)), dma((NC, 4)),
                 dma((NC,)),
                 dma((2 * NC, 5)), dma((2 * NC, 5)), dma((NC, 2)),
                 dma((7,)), dma((7,)),
                 pltpu.SemaphoreType.REGULAR((2,)),
+                smem((1, 1, KMAX), jnp.int32),
             ],
             compiler_params=pltpu.CompilerParams(
                 collective_id=0, has_side_effects=True, vmem_limit_bytes=48 << 20
             ),
         )(*[
-            a if i in (2, 3) else pltpu.with_memory_space_constraint(a, pltpu.HBM)
+            a if i == 3 else pltpu.with_memory_space_constraint(a, pltpu.HBM)
             for i, a in enumerate(operands)
         ])
 

time: 100 us -> 96.8 us (0.968)
  Pallas kernels: 97.2 us -> 93.7 us
    pallas_call x1, Pallas kernels: 97.2 us -> 93.7 us  [local(): pl.pallas_call(functools.partial(kernel, scale), out_shape=(jax.ShapeDtyp...]
where the time goes in v3:
time: 96.8 us; the launch traced here: 96.7 us
  Pallas kernels  93.7 us (97%)
  local copies, waits for them, and re-layouts  1.63 us (2%)
  between operations  1.29 us (1%)
    pallas_call x1, Pallas kernels, local(): pl.pallas_call(functools.partial(kernel, scale), out_shape=(jax.ShapeDtyp...  93.7 us

profile of v3, /device:TPU:1, one launch (start us, length us, event | category | flops | bytes accessed | tf_op | source)
XLA Modules:
  0.0 96.7 jit_solution(908596236381729604)
XLA Ops:
  1.3 93.7 %shard_map.77 = (bf16[128,512]{1,0:T(8,128)(2,1)S(1)}, f32[512,512]{1,0:T(8,128)S(1)}) custom-call(bf16[128,512]{1,0:T(8,128)(2,1)} %features.1, bf16[1,1,6,256,256]{4,3,2,1,0:T(8,128)(2,1)} %tiles.1, s32[1,1,6]{2,1,0:T(1,128)} %index_in.1, s32[1,1]{1,0:T(1,128)S(6)} %copy.10.count, bf16[512,512]{1,0:T(8,128)(2,1)} %weight.1, bf16[128,512]{1,0:T(8,128)(2,1)} %cotangent.1), custom_call_target="tpu_custom_call" | custom-call | tf_op jit(solution)/shard_map/pallas_call | solution.py:399
  95.0 0.7 copy.11
  95.7 1.0 %copy.12 = f32[512,512]{1,0:T(8,128)} copy(f32[512,512]{1,0:T(8,128)S(1)} %get-tuple-element.5) | data formatting | bytes 2097152

commit v4 on v3

--- a/solution.py
+++ b/solution.py
@@ -99,9 +99,9 @@
     y_right, y_left = at(y_=turn(y, 1)), at(y_=turn(y, 3))
 
     barrier = pltpu.get_barrier_semaphore()
-    near = [sibling, x_right, x_left, y_right, y_left] + [at_z(z + 16 + d) for d in (1, -1, 2, -2, 3, -3)]
+    near = [sibling, x_right, x_left, y_right, y_left] + [at_z(z + 16 + d) for d in (3, -3, 2, -2, 1, -1)]
     near += [at(x_=turn(x, d), core_=other) for d in (1, 3)] + [at(z_lo_=turn(z_lo, d), core_=other) for d in (1, 2, 3)]
-    for device in near:
+    for device in near[::-1]:
         pl.semaphore_signal(barrier, inc=1, device_id=device, device_id_type=MESH)
 
     own = [pltpu.make_async_copy(features, staged, s_local.at[0])]
@@ -150,11 +150,11 @@
         give(j, p, s_r.at[j, d], x_left)
 
     def gather_start(j):
-        for d in (1, 3, 2):
+        for d in (2, 3, 1):
             give_own(j, s_z.at[j, 4 - d], at(z_lo_=turn(z_lo, d)), at(z_lo_=turn(z_lo, d), core_=other))
 
-    def gather_z(j):
-        for d in range(1, 4):
+    def gather_z(j, part=(1, 2, 3)):
+        for d in part:
             arrived(got[j].at[turn(z_lo, d) * 4 + x], s_z.at[j, d])
             spread(j, d)
 

time: 96.8 us -> 95.7 us (0.989)
  Pallas kernels: 93.7 us -> 92.6 us
    pallas_call x1, Pallas kernels: 93.7 us -> 92.6 us  [local(): pl.pallas_call(functools.partial(kernel, scale), out_shape=(jax.ShapeDtyp...]
where the time goes in v4:
time: 95.7 us; the launch traced here: 95.5 us
  Pallas kernels  92.6 us (97%)
  local copies, waits for them, and re-layouts  1.63 us (2%)
  between operations  1.29 us (1%)
    pallas_call x1, Pallas kernels, local(): pl.pallas_call(functools.partial(kernel, scale), out_shape=(jax.ShapeDtyp...  92.6 us

profile of v4, /device:TPU:1, one launch (start us, length us, event | category | flops | bytes accessed | tf_op | source)
XLA Modules:
  0.0 95.5 jit_solution(11615830230966924343)
XLA Ops:
  1.3 92.6 %shard_map.77 = (bf16[128,512]{1,0:T(8,128)(2,1)S(1)}, f32[512,512]{1,0:T(8,128)S(1)}) custom-call(bf16[128,512]{1,0:T(8,128)(2,1)} %features.1, bf16[1,1,6,256,256]{4,3,2,1,0:T(8,128)(2,1)} %tiles.1, s32[1,1,6]{2,1,0:T(1,128)} %index_in.1, s32[1,1]{1,0:T(1,128)S(6)} %copy.10.count, bf16[512,512]{1,0:T(8,128)(2,1)} %weight.1, bf16[128,512]{1,0:T(8,128)(2,1)} %cotangent.1), custom_call_target="tpu_custom_call" | custom-call | tf_op jit(solution)/shard_map/pallas_call | solution.py:399
  93.9 0.7 copy.11
  94.5 1.0 %copy.12 = f32[512,512]{1,0:T(8,128)} copy(f32[512,512]{1,0:T(8,128)S(1)} %get-tuple-element.5) | data formatting | bytes 2097152

commit v5 on v4

--- a/solution.py
+++ b/solution.py
@@ -353,7 +353,7 @@
     for i in range(1, 16):
         total = total + z_in[i].astype(F32)
     z_all[z_lo] = total.astype(BF16)
-    for d in range(1, 4):
+    for d in (2, 3, 1):
         remote(z_all.at[z_lo], z_all.at[z_lo], s_gsend.at[4], s_grecv.at[4], at(z_lo_=turn(z_lo, d)))
     arrived(z_all.at[pl.ds(0, 3)], s_grecv.at[4])
     full[core, chip_xy] = z_all[...]

time: 95.7 us -> 95.9 us (level)
  no operation moved by 1% of the time
where the time goes in v5:
time: 95.9 us; the launch traced here: 95.7 us
  Pallas kernels  92.7 us (97%)
  local copies, waits for them, and re-layouts  1.63 us (2%)
  between operations  1.29 us (1%)
    pallas_call x1, Pallas kernels, local(): pl.pallas_call(functools.partial(kernel, scale), out_shape=(jax.ShapeDtyp...  92.7 us

profile of v5, /device:TPU:1, one launch (start us, length us, event | category | flops | bytes accessed | tf_op | source)
XLA Modules:
  0.0 95.7 jit_solution(13774067246089493570)
XLA Ops:
  1.3 92.7 %shard_map.77 = (bf16[128,512]{1,0:T(8,128)(2,1)S(1)}, f32[512,512]{1,0:T(8,128)S(1)}) custom-call(bf16[128,512]{1,0:T(8,128)(2,1)} %features.1, bf16[1,1,6,256,256]{4,3,2,1,0:T(8,128)(2,1)} %tiles.1, s32[1,1,6]{2,1,0:T(1,128)} %index_in.1, s32[1,1]{1,0:T(1,128)S(6)} %copy.10.count, bf16[512,512]{1,0:T(8,128)(2,1)} %weight.1, bf16[128,512]{1,0:T(8,128)(2,1)} %cotangent.1), custom_call_target="tpu_custom_call" | custom-call | tf_op jit(solution)/shard_map/pallas_call | solution.py:399
  94.0 0.7 copy.11
  94.7 1.0 %copy.12 = f32[512,512]{1,0:T(8,128)} copy(f32[512,512]{1,0:T(8,128)S(1)} %get-tuple-element.5) | data formatting | bytes 2097152
